TPU v7x, 32 devices: a whole 2x2x4 slice. The times are simulated.
32 devices in a mesh: tok: 8 (over z, y), wa: 2 (over x), wb: 2 (over core).
Axes of the slice: x: 2, y: 2, z: 4, core: 2. Of those that a mesh axis runs over, the one named last changes fastest.
Arguments:
- tokens: bfloat16 [4096, 1024], P(('tok', 'wa', 'wb')), may hold values from -6 to 6
- deal: int32 [4096], P(('tok', 'wa', 'wb')), may hold values from 0 to 4095, as said below
- lengths: int32 [8, 8], P('tok'), may hold values from 1 to 192, 512 in all within a row
- group_ids: int32 [8, 8], P('tok'), may hold values from 0 to 1
- page_table: int32 [2, 4], replicated, may hold values from 0 to 15, as said below
- prefix_cache: bfloat16 [16, 128, 2, 1024], P('tok', None, None, ('wa', 'wb')), may hold values from -12 to 12
- qkv_weight: bfloat16 [1024, 3, 1024], P(None, None, ('wa', 'wb')), may hold values from -0.1875 to 0.1875
- qkv_bias: float32 [3, 1024], P(None, ('wa', 'wb')), may hold values from -9 to 9
- out_weight: bfloat16 [1024, 1024], P(('wa', 'wb')), may hold values from -9 to 9
- out_bias: float32 [1024], replicated, may hold values from -3 to 3
- norm1_gain: float32 [1024], replicated, may hold values from 0.5 to 1.5
- norm1_bias: float32 [1024], replicated, may hold values from -3 to 3
- up_weight: bfloat16 [1024, 4096], P(None, ('wa', 'wb')), may hold values from -0.1875 to 0.1875
- up_bias: float32 [4096], P(('wa', 'wb')), may hold values from -3 to 3
- down_weight: bfloat16 [4096, 1024], P(('wa', 'wb')), may hold values from -0.09375 to 0.09375
- down_bias: float32 [1024], replicated, may hold values from -3 to 3
- norm2_gain: float32 [1024], replicated, may hold values from 0.5 to 1.5
- norm2_bias: float32 [1024], replicated, may hold values from -3 to 3
Outputs:
- hidden: bfloat16 [4096, 1024], P(('tok', 'wa', 'wb'))
- suffix_cache: bfloat16 [4096, 2, 1024], P('tok', None, ('wa', 'wb'))
Inputs may be any that keep to these rules, and one draw needn't show every extreme that they name: deal is a permutation of 0 to 4095. For the device at index r of tok and index c of the joined wa+wb axis, its 128 entries are, in some order, (s * 4 + c) * 128 + r * 16 + k over all s < 8 and k < 16. Every row of lengths sums to 512. `page_table`: all entries are distinct slots; slots 0 and 15 are always used. Slot s is held by index s // 2 of tok; one index holds 2 live slots.
All inputs are finite; a program needn't handle non-finite values.
Results may differ from a plain program's by a relative error of at most 0.015.
Values may be sent and summed in bfloat16 or wider, within the bound.
A program may use at most 128 MiB of HBM per device.

v0:
```python
import math

import jax
import jax.numpy as jnp
from jax import lax
from jax.sharding import PartitionSpec as P

HEAD = 64
SEQ_DEV = 8


def layer_norm(values, gain, bias):
    mean = jnp.mean(values, axis=-1, keepdims=True)
    centered = values - mean
    spread = jnp.mean(centered * centered, axis=-1, keepdims=True)
    return centered * lax.rsqrt(spread + 1e-05) * gain + bias


def widen(rows, weight, bias):
    return (
        jnp.dot(
            lax.all_gather(rows, ("wa", "wb"), axis=0, tiled=True),
            weight,
            preferred_element_type=jnp.float32,
        )
        + bias
    )


def narrow(values, weight):
    return lax.psum_scatter(
        jnp.dot(values, weight, preferred_element_type=jnp.float32).astype(jnp.bfloat16),
        ("wa", "wb"),
        scatter_dimension=0,
        tiled=True,
    ).astype(jnp.float32)


def local(
    tokens,
    deal,
    lengths,
    group_ids,
    page_table,
    prefix_cache,
    qkv_weight,
    qkv_bias,
    out_weight,
    out_bias,
    norm1_gain,
    norm1_bias,
    up_weight,
    up_bias,
    down_weight,
    down_bias,
    norm2_gain,
    norm2_bias,
):
    scale = 1.0 / math.sqrt(HEAD)
    tok_count = lax.axis_size("tok")
    block_devs = lax.axis_size("wa") * lax.axis_size("wb")
    row_dev, width = tokens.shape
    run_len = row_dev // tok_count
    arrived = lax.all_to_all(
        tokens.reshape(tok_count, run_len, width), "tok", split_axis=0, concat_axis=0, tiled=True
    ).reshape(row_dev, width)
    source = deal // (block_devs * row_dev) * run_len + deal % run_len
    ordered = jnp.take(arrived, source, axis=0)
    quarter = qkv_weight.shape[2]
    heads_dev = quarter // HEAD
    qkv = widen(
        ordered, qkv_weight.reshape(width, 3 * quarter), qkv_bias.reshape(3 * quarter)
    ).astype(jnp.bfloat16)
    tok_dev = qkv.shape[0]
    qkv = qkv.reshape(tok_dev, 3, quarter)
    cache_out = qkv[:, 1:3, :]
    queries = qkv[:, 0].reshape(tok_dev, heads_dev, HEAD)
    keys = qkv[:, 1].reshape(tok_dev, heads_dev, HEAD)
    values = qkv[:, 2].reshape(tok_dev, heads_dev, HEAD)
    ends = jnp.cumsum(lengths[0])
    places = jnp.arange(tok_dev, dtype=jnp.int32)
    seq = jnp.sum((places[:, None] >= ends[None, :]).astype(jnp.int32), axis=1)
    seq_ids = jnp.arange(SEQ_DEV, dtype=jnp.int32)
    row_group = jnp.sum(
        jnp.where(seq[:, None] == seq_ids[None, :], group_ids[0][None, :], 0), axis=1
    )
    allowed = (seq[:, None] == seq[None, :]) & (places[None, :] <= places[:, None])
    near = jnp.einsum("qhd,khd->hqk", queries, keys, preferred_element_type=jnp.float32) * scale
    near = jnp.where(allowed[None], near, -jnp.inf)
    best = jnp.max(near, axis=2)
    near_weight = jnp.exp(near - best[:, :, None])
    total = jnp.sum(near_weight, axis=2)
    accum = jnp.einsum(
        "hqk,khd->hqd", near_weight.astype(jnp.bfloat16), values, preferred_element_type=jnp.float32
    )
    pool_size = tok_count * prefix_cache.shape[0]
    page_len = prefix_cache.shape[1]
    slot_ids = jnp.arange(pool_size, dtype=jnp.int32)
    matches = (page_table[:, :, None] == slot_ids[None, None, :]).astype(jnp.int32)
    hits = jnp.sum(matches, axis=1)
    group_range = jnp.arange(page_table.shape[0], dtype=jnp.int32)
    owner_group = jnp.sum(hits * group_range[:, None], axis=0)
    slot_group = jnp.where(jnp.sum(hits, axis=0) > 0, owner_group, -1)
    piece = lax.all_gather(prefix_cache, "tok", axis=0, tiled=True)
    count = piece.shape[0]
    step = math.gcd(count, 8)
    blocks = count // step
    unused_slot = (slot_group < 0).astype(jnp.int32)
    live_first = jnp.argsort(unused_slot, stable=True)
    live_count = count - jnp.sum(unused_slot)
    sorted_groups = jnp.take(slot_group, live_first, axis=0)

    def one_block(carry, index):

        def compute(carry_in):
            top, weight_sum, summed = carry_in
            picks = lax.dynamic_slice_in_dim(live_first, index * step, step, 0)
            pair = jnp.take(piece, picks, axis=0).reshape(step * page_len, 2, heads_dev, HEAD)
            block_groups = lax.dynamic_slice_in_dim(sorted_groups, index * step, step, 0)
            groups = jnp.broadcast_to(block_groups[:, None], (step, page_len)).reshape(
                step * page_len
            )
            far = (
                jnp.einsum("qhd,khd->hqk", queries, pair[:, 0], preferred_element_type=jnp.float32)
                * scale
            )
            far = jnp.where((groups[None, :] == row_group[:, None])[None], far, -jnp.inf)
            new_top = jnp.maximum(top, jnp.max(far, axis=2))
            factor = jnp.exp(top - new_top)
            far_weight = jnp.exp(far - new_top[:, :, None])
            weight_sum = weight_sum * factor + jnp.sum(far_weight, axis=2)
            summed = summed * factor[:, :, None] + jnp.einsum(
                "hqk,khd->hqd",
                far_weight.astype(jnp.bfloat16),
                pair[:, 1],
                preferred_element_type=jnp.float32,
            )
            return (new_top, weight_sum, summed)

        def keep(carry_in):
            return carry_in

        return (lax.cond(index * step < live_count, compute, keep, carry), None)

    result, unused = lax.scan(one_block, (best, total, accum), jnp.arange(blocks, dtype=jnp.int32))
    best, total, accum = result
    attention = (
        (accum / total[:, :, None])
        .transpose(1, 0, 2)
        .reshape(tok_dev, quarter)
        .astype(jnp.bfloat16)
    )
    mixed = narrow(attention, out_weight) + out_bias + ordered.astype(jnp.float32)
    normed = layer_norm(mixed, norm1_gain, norm1_bias).astype(jnp.bfloat16)
    raised = widen(normed, up_weight, up_bias)
    inner = jax.nn.gelu(raised, approximate=False).astype(jnp.bfloat16)
    outer = narrow(inner, down_weight) + down_bias + normed.astype(jnp.float32)
    hidden = layer_norm(outer, norm2_gain, norm2_bias).astype(jnp.bfloat16)
    return (hidden, cache_out)


def solution(mesh):
    return jax.shard_map(
        local,
        mesh=mesh,
        in_specs=(
            P(("tok", "wa", "wb"), None),
            P(("tok", "wa", "wb")),
            P("tok", None),
            P("tok", None),
            P(),
            P("tok", None, None, ("wa", "wb")),
            P(None, None, ("wa", "wb")),
            P(None, ("wa", "wb")),
            P(("wa", "wb"), None),
            P(),
            P(),
            P(),
            P(None, ("wa", "wb")),
            P(("wa", "wb")),
            P(("wa", "wb"), None),
            P(),
            P(),
            P(),
        ),
        out_specs=(P(("tok", "wa", "wb"), None), P("tok", None, ("wa", "wb"))),
        check_vma=False,
    )
```

profile of v0, /device:TPU:0, one launch (start us, length us, event | category | flops | bytes accessed | tf_op | source)
XLA Modules:
  0.0 211.3 jit_solution(2733800110980042349)
XLA Ops:
  7.2 7.4 %all-to-all-start = ((bf16[8,16,1024]{2,1,0:T(8,128)(2,1)}), bf16[8,16,1024]{2,1,0:T(8,128)(2,1)S(1)}, u32[]{:S(2)}, u32[]{:S(2)}) async-start(bf16[8,16,1024]{2,1,0:T(8,128)(2,1)} %bitcast.62), calls=%async_computation | async-start | bytes 524288 | tf_op jit(solution)/shard_map/all_to_all | solution.py:64
  15.4 8.2 %all-to-all-done = bf16[8,16,1024]{2,1,0:T(8,128)(2,1)S(1)} async-done(((bf16[8,16,1024]{2,1,0:T(8,128)(2,1)}), bf16[8,16,1024]{2,1,0:T(8,128)(2,1)S(1)}, u32[]{:S(2)}, u32[]{:S(2)}) %all-to-all-start) | async-done | bytes 262176 | tf_op jit(solution)/shard_map/all_to_all | solution.py:64
  26.1 2.6 %copy.42 = bf16[1024,3,256]{0,2,1:T(8,128)(2,1)} copy(bf16[1024,3,256]{2,0,1:T(8,128)(2,1)} %param.28) | data formatting | bytes 3145728 | tf_op args[6]
  32.6 9.2 %all-gather.4.cloned.1.call-done = bf16[512,1024]{1,0:T(8,128)(2,1)} async-done(((bf16[128,1024]{1,0:T(8,128)(2,1)}), bf16[512,1024]{1,0:T(8,128)(2,1)}) %all-gather.4.cloned.1.call-update) | async-done | bytes 1048592 | tf_op jit(solution)/shard_map/all_gather | solution.py:22
  41.8 3.7 %add_convert_fusion = bf16[512,768]{1,0:T(8,128)(2,1)} fusion(bf16[512,1024]{1,0:T(8,128)(2,1)} %all-gather.4.cloned.1.call-done, bf16[1024,768]{0,1:T(8,128)(2,1)} %bitcast.57, f32[768]{0:T(1024)S(1)} %add.119), kind=kOutput, calls=%fused_computation.51 | convolution fusion | flops 806092800 | bytes 3410944 | tf_op jit(solution)/shard_map/dot_general | solution.py:21
  47.9 2.1 fusion.24
  50.9 42.3 %all-gather.6.cloned.1.call-done = bf16[16,128,2,256]{3,1,2,0:T(8,128)(2,1)} async-done(((bf16[2,128,2,256]{3,1,2,0:T(8,128)(2,1)}), bf16[16,128,2,256]{3,1,2,0:T(8,128)(2,1)}) %all-gather.6.cloned.1.call-update) | async-done | bytes 2097168 | tf_op jit(solution)/shard_map/all_gather | solution.py:104
  93.2 5.1 %copy.46 = bf16[16,128,2,256]{3,2,1,0:T(2,128)(2,1)} copy(bf16[16,128,2,256]{3,1,2,0:T(8,128)(2,1)} %all-gather.6.cloned.1.call-done) | data formatting | bytes 4194304 | tf_op jit(solution)/shard_map/while | solution.py:145
  98.3 19.6 %while.14 = (s32[]{:T(128)}, f32[4,512]{1,0:T(4,128)S(1)}, f32[4,512]{1,0:T(4,128)S(1)}, f32[4,512,64]{1,2,0:T(8,128)}, s32[2]{0:T(128)S(1)}, /*index=5*/s32[]{:...) while((s32[]{:T(128)}, f32[4,512]{1,0:T(4,128)S(1)}, ...), condition=%wide.region_15.16_spmd, body=%wide.region_10.15_spmd.sunk | while | flops 561255488 | bytes 39207528 | solution.py:145
  99.4 17.3 %conditional.2 = ((f32[4,512]{1,0:T(4,128)S(1)}, f32[4,512]{1,0:T(4,128)S(1)}, f32[4,512,64]{1,2,0:T(8,128)})) conditional(s32[]{:T(128)} %convert_element_type.124, (f32[4,512]{1,0:T(4,128)S(1)}, f32[4,512]{1,0:T(4,128)S(1)}, f32[4,512,64]{1,2,0:T(8,128)}) %tuple.45, (s32[]{:T(128)}, s32[16]{0:T(128)S(1)}, s32[512]{0:T(512)S(1)}, ...), branch_computations={%region_11.11_spmd, %region_12.14_spmd} | conditional | flops 561255488 | bytes 39207264 | solution.py:143
  100.3 4.2 %gather_fusion = bf16[8,128,2,256]{3,2,1,0:T(2,128)(2,1)S(1)} fusion(bf16[16,128,2,256]{3,2,1,0:T(2,128)(2,1)} %get-tuple-element.73, s32[1024]{0:T(1024)S(1)} %pad_clamp_fusion), kind=kCustom, calls=%fused_computation | custom fusion | bytes 2097184 | tf_op jit(solution)/shard_map/while/body/eval_jaxpr/cond/branch_1_fun/jit(_take)/gather | solution.py:118
  104.6 2.2 %copy.40 = bf16[8,128,2,256]{1,0,3,2:T(8,128)(2,1)} copy(bf16[8,128,2,256]{3,2,1,0:T(2,128)(2,1)S(1)} %gather_fusion) | data formatting | bytes 2097152 | tf_op jit(solution)/shard_map/while/body/eval_jaxpr/cond/branch_1_fun/jit(_take)/gather | solution.py:118
  106.8 1.5 gather.11
  109.3 1.6 fusion.2
  110.9 1.8 fusion.1
  112.7 4.0 %fusion.6 = f32[4,512,64]{1,2,0:T(8,128)} fusion(f32[4,1024,512]{2,1,0:T(8,128)S(1)} %get-tuple-element.161, f32[4,512]{1,0:T(4,128)S(1)} %max.2, pred[512,1024]{0,1:T(8,128)(4,1)S(1)} %broadcast_compare_fusion, bf16[1024,2,4,64]{0,3,2,1:T(8,128)(2,1)S(1)} %broadcast_select_fusion, f32[4,512,64]{1,2,0:T(8,128)} %get-tuple-element.76, ...), kind=kOutput, calls=%fused_computation.10 | convolution fusion | flops 277086208 | bytes 10502144 | tf_op jit(solution)/shard_map/while/body/eval_jaxpr/cond/branch_1_fun/hqk,khd->hqd/dot_general | solution.py:132
  119.0 2.5 %convolution_convert_fusion.1 = bf16[512,1024]{1,0:T(8,128)(2,1)} fusion(bf16[512,256]{0,1:T(8,128)(2,1)S(1)} %bitcast.58, bf16[256,1024]{1,0:T(8,128)(2,1)} %param.30), kind=kOutput, calls=%fused_computation.53 | convolution fusion | flops 268959744 | bytes 1835008 | tf_op jit(solution)/shard_map/dot_general | solution.py:32
  121.6 23.5 %reduce-scatter.3.cloned.1.call-done = bf16[128,1024]{1,0:T(8,128)(2,1)} async-done(((bf16[512,1024]{1,0:T(8,128)(2,1)}), bf16[128,1024]{1,0:T(8,128)(2,1)}) %reduce-scatter.3.cloned.1.call-update) | async-done | bytes 262160 | tf_op jit(solution)/shard_map/reduce_scatter | solution.py:31
  147.5 1.9 add_convert_fusion.2
  149.7 16.6 %all-gather.8.cloned.1.call-done = bf16[512,1024]{1,0:T(8,128)(2,1)} async-done(((bf16[128,1024]{1,0:T(8,128)(2,1)}), bf16[512,1024]{1,0:T(8,128)(2,1)}) %all-gather.8.cloned.1.call-update) | async-done | bytes 1048592 | tf_op jit(solution)/shard_map/all_gather | solution.py:22
  166.3 9.2 %convolution_convert_fusion = bf16[512,1024]{1,0:T(8,128)(2,1)} fusion(bf16[1024,1024]{1,0:T(8,128)(2,1)S(1)} %copy-done, bf16[512,1024]{1,0:T(8,128)(2,1)} %all-gather.8.cloned.1.call-done, bf16[1024,1024]{1,0:T(8,128)(2,1)} %param.34, f32[1024]{0:T(1024)S(1)} %copy-done.16), kind=kOutput, calls=%fused_computation.52 | convolution fusion | flops 2182610944 | bytes 6295552 | tf_op jit(solution)/shard_map/dot_general | solution.py:32
  176.4 2.0 copy.47
  178.4 22.2 %reduce-scatter.5.cloned.1.call-done = bf16[128,1024]{1,0:T(8,128)(2,1)} async-done(((bf16[512,1024]{1,0:T(8,128)(2,1)}), bf16[128,1024]{1,0:T(8,128)(2,1)}) %reduce-scatter.5.cloned.1.call-update) | async-done | bytes 262160 | tf_op jit(solution)/shard_map/reduce_scatter | solution.py:31
  202.9 1.8 add_convert_fusion.1
  (94 shorter events, 19.2 us)
Async XLA Ops:
  7.2 159.2 %copy-start = (bf16[1024,1024]{1,0:T(8,128)(2,1)S(1)}, bf16[1024,1024]{1,0:T(8,128)(2,1)}, u32[]{:S(2)}) copy-start(bf16[1024,1024]{1,0:T(8,128)(2,1)} %param.36) | copy-start | bytes 6291460
  7.2 18.1 %copy-start.6 = (bf16[2,128,2,256]{3,2,1,0:T(2,128)(2,1)S(1)}, bf16[2,128,2,256]{3,2,1,0:T(2,128)(2,1)}, u32[]{:S(2)}) copy-start(bf16[2,128,2,256]{3,2,1,0:T(2,128)(2,1)} %param.27) | copy-start | bytes 786436
  7.2 16.3 %all-to-all-start = ((bf16[8,16,1024]{2,1,0:T(8,128)(2,1)}), bf16[8,16,1024]{2,1,0:T(8,128)(2,1)S(1)}, u32[]{:S(2)}, u32[]{:S(2)}) async-start(bf16[8,16,1024]{2,1,0:T(8,128)(2,1)} %bitcast.62), calls=%async_computation | async-start | bytes 524288 | tf_op jit(solution)/shard_map/all_to_all | solution.py:64
  14.6 11.5 %copy-start.13 = (f32[3,256]{1,0:T(4,128)S(1)}, f32[3,256]{1,0:T(4,128)}, u32[]{:S(2)}) copy-start(f32[3,256]{1,0:T(4,128)} %param.29) | copy-start | bytes 9220
  14.6 27.2 %all-gather.4.cloned.1.call-start = ((), (), s32[]{:S(2)}) async-start(), calls=%async_computation.3 | async-start | bytes 1310720 | tf_op jit(solution)/shard_map/all_gather | solution.py:22
  25.2 3.5 %copy-start.17 = (s32[1,8]{1,0:T(1,128)S(1)}, s32[1,8]{1,0:T(1,128)}, u32[]{:S(2)}) copy-start(s32[1,8]{1,0:T(1,128)} %param.24) | copy-start | bytes 100
  25.2 3.7 %copy-start.14 = (s32[2,4]{1,0:T(2,128)S(1)}, s32[2,4]{1,0:T(2,128)}, u32[]{:S(2)}) copy-start(s32[2,4]{1,0:T(2,128)} %param.26) | copy-start | bytes 100
  25.2 68.0 %all-gather.6.cloned.1.call-start = ((), (), s32[]{:S(2)}) async-start(), calls=%async_computation.4 | async-start | bytes 2359296 | tf_op jit(solution)/shard_map/all_gather | solution.py:104
  26.0 6.3 %copy-start.15 = (s32[1,8]{1,0:T(1,128)S(1)}, s32[1,8]{1,0:T(1,128)}, u32[]{:S(2)}) copy-start(s32[1,8]{1,0:T(1,128)} %param.25) | copy-start | bytes 100
  26.0 119.0 %reduce-scatter.3.cloned.1.call-start = ((), (), s32[]{:S(2)}) async-start(), calls=%async_computation.5 | async-start | bytes 1310720 | tf_op jit(solution)/shard_map/reduce_scatter | solution.py:31
  46.9 1.0 copy-start.2
  47.0 0.9 copy-start.4
  108.3 1.0 copy-start.5
  117.9 27.2 %copy-start.7 = (f32[1024]{0:T(1024)S(1)}, f32[1024]{0:T(1024)}, u32[]{:S(2)}) copy-start(f32[1024]{0:T(1024)} %param.31) | copy-start | bytes 12292
  119.0 28.5 %copy-start.9 = (f32[1024]{0:T(1024)S(1)}, f32[1024]{0:T(1024)}, u32[]{:S(2)}) copy-start(f32[1024]{0:T(1024)} %param.33) | copy-start | bytes 12292
  119.0 28.5 %copy-start.10 = (f32[1024]{0:T(1024)S(1)}, f32[1024]{0:T(1024)}, u32[]{:S(2)}) copy-start(f32[1024]{0:T(1024)} %param.32) | copy-start | bytes 12292
  119.0 47.3 %copy-start.16 = (f32[1024]{0:T(1024)S(1)}, f32[1024]{0:T(1024)}, u32[]{:S(2)}) copy-start(f32[1024]{0:T(1024)} %param.35) | copy-start | bytes 12292
  121.6 44.8 %all-gather.8.cloned.1.call-start = ((), (), s32[]{:S(2)}) async-start(), calls=%async_computation.6 | async-start | bytes 1310720 | tf_op jit(solution)/shard_map/all_gather | solution.py:22
  149.4 26.2 %copy-start.3 = (bf16[512,768]{0,1:T(8,128)(2,1)S(1)}, bf16[512,768]{0,1:T(8,128)(2,1)}, u32[]{:S(2)}) copy-start(bf16[512,768]{0,1:T(8,128)(2,1)} %copy-done.2) | copy-start | bytes 2359300
  149.4 51.2 %reduce-scatter.5.cloned.1.call-start = ((), (), s32[]{:S(2)}) async-start(), calls=%async_computation.7 | async-start | bytes 1310720 | tf_op jit(solution)/shard_map/reduce_scatter | solution.py:31
  175.5 25.1 %copy-start.1 = (bf16[128,1024]{1,0:T(8,128)(2,1)S(1)}, bf16[128,1024]{1,0:T(8,128)(2,1)}, u32[]{:S(2)}) copy-start(bf16[128,1024]{1,0:T(8,128)(2,1)} %add_convert_fusion.2) | copy-start | bytes 786436
  175.5 25.1 %copy-start.8 = (f32[1024]{0:T(1024)S(1)}, f32[1024]{0:T(1024)}, u32[]{:S(2)}) copy-start(f32[1024]{0:T(1024)} %param.37) | copy-start | bytes 12292
  175.5 27.4 %copy-start.11 = (f32[1024]{0:T(1024)S(1)}, f32[1024]{0:T(1024)}, u32[]{:S(2)}) copy-start(f32[1024]{0:T(1024)} %param.39) | copy-start | bytes 12292
  175.5 27.4 %copy-start.12 = (f32[1024]{0:T(1024)S(1)}, f32[1024]{0:T(1024)}, u32[]{:S(2)}) copy-start(f32[1024]{0:T(1024)} %param.38) | copy-start | bytes 12292
Sparse Core Ops, SparseCore 0:
  25.3 16.4 all-gather.3
  43.9 49.2 all-gather.5
  121.7 23.3 reduce-scatter.2
  149.6 16.7 all-gather.7
  175.7 24.8 reduce-scatter.4
where the time goes:
time: 212 us; the launch traced here: 211 us
  waiting for transfers between devices  122 us (58%)
  local copies, waits for them, and re-layouts  24.1 us (11%)
  matrix products  24 us (11%)
  other arithmetic  16.9 us (8%)
  between operations  14.6 us (7%)
  starting transfers between devices  7.85 us (4%)
    reduce_scatter x2, waiting for transfers between devices, narrow(): lax.psum_scatter(jnp.dot(values, weight, preferred_element_type=jnp.float...  45.7 us
    all_gather x1, waiting for transfers between devices, local(): piece = lax.all_gather(prefix_cache, 'tok', axis=0, tiled=True)  42.3 us
    all_gather x2, waiting for transfers between devices, widen(): lax.all_gather(rows, ('wa', 'wb'), axis=0, tiled=True)  25.8 us
    dot_general x2, matrix products, narrow(): jnp.dot(values, weight, preferred_element_type=jnp.float32)  11.7 us
    all_to_all x1, waiting for transfers between devices, local(): lax.all_to_all(tokens.reshape(tok_count, run_len, width), 'tok', split_ax...  8.18 us
    gather x3, local copies, waits for them, and re-layouts, compute(): jnp.take(piece, picks, axis=0).reshape(step * page_len, 2, heads_dev, HEAD)  7.97 us
    all_to_all x1, starting transfers between devices, local(): lax.all_to_all(tokens.reshape(tok_count, run_len, width), 'tok', split_ax...  7.42 us
    unnamed x37, local copies, waits for them, and re-layouts  5.41 us
  transfers between devices with their start and end apart: 6, of which 6 were waited for; matrix products, arithmetic and copies ran while one was open for 9% of the time, Pallas kernels for 0%

commit v1 on v0

--- a/solution.py
+++ b/solution.py
@@ -1,12 +1,18 @@
+import functools
 import math
 
 import jax
 import jax.numpy as jnp
 from jax import lax
+from jax.experimental import pallas as pl
+from jax.experimental.pallas import tpu as pltpu
 from jax.sharding import PartitionSpec as P
 
 HEAD = 64
 SEQ_DEV = 8
+MOST_LEN = 192
+FAR = 3e38
+MESH = pl.DeviceIdType.MESH
 
 
 def layer_norm(values, gain, bias):
@@ -36,7 +42,7 @@
     ).astype(jnp.float32)
 
 
-def local(
+def collective_local(
     tokens,
     deal,
     lengths,
@@ -159,9 +165,514 @@
     return (hidden, cache_out)
 
 
+def layer_kernel(
+    n_tok,
+    tokens,
+    deal,
+    lengths,
+    group_ids,
+    page_table,
+    own_kv,
+    qkv_w_hbm,
+    qkv_b,
+    out_w_hbm,
+    out_b,
+    gain1,
+    bias1,
+    up_w_hbm,
+    up_b,
+    down_w_hbm,
+    down_b,
+    gain2,
+    bias2,
+    hidden,
+    kv_out,
+    qkv_w,
+    out_w,
+    up_w,
+    down_w,
+    arrived,
+    x_all,
+    kv_all,
+    far_k,
+    far_v,
+    queries,
+    attended,
+    part_send,
+    part_recv,
+    wide_send,
+    wide_recv,
+    n_all,
+    kept,
+    w_sem,
+    deal_s,
+    deal_r,
+    kv_s,
+    kv_r,
+    x_s,
+    x_r,
+    p_s,
+    p_r,
+    n_s,
+    n_r,
+):
+    tok = lax.axis_index("tok")
+    a = lax.axis_index("wa")
+    b = lax.axis_index("wb")
+    rows, width = tokens.shape
+    run = rows // n_tok
+    quarter = qkv_b.shape[1] // 3
+    heads = quarter // HEAD
+    groups, pages = page_table.shape
+    page_len = own_kv.shape[2]
+    far_len = pages * page_len
+    depth = n_tok // 2
+    z, y = tok // 2, tok % 2
+    own = a * 2 + b
+    near_core = a * 2 + (1 - b)
+    across = (1 - a) * 2 + b
+    corner = (1 - a) * 2 + (1 - b)
+    core_peer = (tok, a, 1 - b)
+    x_peer = (tok, 1 - a, b)
+
+    loads = [
+        pltpu.make_async_copy(src, dst, w_sem.at[i])
+        for i, (src, dst) in enumerate(
+            ((qkv_w_hbm, qkv_w), (out_w_hbm, out_w), (up_w_hbm, up_w), (down_w_hbm, down_w))
+        )
+    ]
+    for load in loads:
+        load.start()
+
+    barrier = pltpu.get_barrier_semaphore()
+    for d in range(1, n_tok):
+        pl.semaphore_signal(
+            barrier, inc=1, device_id=(lax.rem(tok + d, n_tok), a, b), device_id_type=MESH
+        )
+    for peer in (core_peer, x_peer):
+        pl.semaphore_signal(barrier, inc=1, device_id=peer, device_id_type=MESH)
+    pl.semaphore_wait(barrier, n_tok + 1)
+
+    def remote(src, dst, send_sem, recv_sem, peer):
+        return pltpu.make_async_remote_copy(
+            src_ref=src,
+            dst_ref=dst,
+            send_sem=send_sem,
+            recv_sem=recv_sem,
+            device_id=peer,
+            device_id_type=MESH,
+        )
+
+    def run_at(index):
+        return pl.ds(pl.multiple_of(index * run, run), run)
+
+    deals = []
+    for d in range(1, n_tok):
+        to = lax.rem(tok + d, n_tok)
+        copy = remote(
+            tokens.at[run_at(to)], arrived.at[run_at(tok)], deal_s.at[d], deal_r.at[d], (to, a, b)
+        )
+        copy.start()
+        deals.append(copy)
+
+    RIGHT, LEFT, PAIR = 0, 1, 2
+
+    def kv_peer(way):
+        if way == PAIR:
+            return (z * 2 + (1 - y), a, b)
+        step = 1 if way == RIGHT else -1
+        return ((z + step) * 2 + y, a, b)
+
+    def kv_copy(source, slot, way, from_own):
+        held = kv_all.at[source, slot]
+        return remote(
+            own_kv.at[slot] if from_own else held,
+            held,
+            kv_s.at[source, slot, way],
+            kv_r.at[source, slot],
+            kv_peer(way),
+        )
+
+    def kv_each(source, slot, ways, action, from_own=False):
+        for way in ways:
+            if way == PAIR:
+                action(kv_copy(source, slot, way, from_own))
+            else:
+
+                @pl.when((z < depth - 1) if way == RIGHT else (z > 0))
+                def _():
+                    action(kv_copy(source, slot, way, from_own))
+
+    def begin(copy):
+        copy.start()
+
+    def sent(copy):
+        copy.wait_send()
+
+    def kv_arrived(source, slot):
+        kv_copy(source, slot, PAIR, False).wait_recv()
+
+    other = z * 2 + (1 - y)
+    kv_each(tok, 1, (PAIR,), begin, True)
+    kv_each(tok, 0, (RIGHT, LEFT), begin, True)
+    kv_each(tok, 1, (RIGHT, LEFT), begin, True)
+    kv_each(tok, 0, (PAIR,), begin, True)
+    kv_all[tok] = own_kv[...]
+
+    def kv_step(distance):
+        if distance == 0:
+            kv_arrived(other, 1)
+            kv_each(other, 1, (RIGHT, LEFT), begin)
+            return
+        for way, base in ((RIGHT, z - distance), (LEFT, z + distance)):
+
+            @pl.when((base >= 0) & (base < depth))
+            def _():
+                same, cross = base * 2 + y, base * 2 + (1 - y)
+                kv_arrived(same, 0)
+                kv_each(same, 0, (way, PAIR), begin)
+                kv_arrived(same, 1)
+                kv_each(same, 1, (way,), begin)
+                kv_arrived(cross, 1)
+                kv_each(cross, 1, (way,), begin)
+
+    def kv_finish():
+        for base in range(depth):
+            kv_arrived(base * 2 + (1 - y), 0)
+        kv_each(tok, 0, (RIGHT, LEFT, PAIR), sent, True)
+        kv_each(tok, 1, (RIGHT, LEFT, PAIR), sent, True)
+        kv_each(other, 1, (RIGHT, LEFT), sent)
+        for distance in range(1, depth):
+            for way, base in ((RIGHT, z - distance), (LEFT, z + distance)):
+
+                @pl.when((base >= 0) & (base < depth))
+                def _():
+                    same, cross = base * 2 + y, base * 2 + (1 - y)
+                    kv_each(same, 0, (way, PAIR), sent)
+                    kv_each(same, 1, (way,), sent)
+                    kv_each(cross, 1, (way,), sent)
+
+    arrived[run_at(tok)] = tokens[run_at(tok)]
+    places = deal[...]
+    source = places // (4 * rows) * run + lax.rem(places, run)
+    hot = jnp.where(
+        lax.broadcasted_iota(jnp.int32, (rows, rows), 0) == jnp.broadcast_to(source, (rows, rows)),
+        1.0,
+        0.0,
+    )
+    pick = hot.T.astype(jnp.bfloat16)
+    for copy in deals:
+        copy.wait_recv()
+    x_all[own] = jnp.dot(pick, arrived[...], preferred_element_type=jnp.float32).astype(
+        jnp.bfloat16
+    )
+
+    half = rows // 2
+
+    def spread(buffer, send_sems, recv_sems):
+        outs = []
+        for part in range(2):
+            piece = pl.ds(part * half, half)
+            outs.append(
+                remote(
+                    buffer.at[own, piece],
+                    buffer.at[own, piece],
+                    send_sems.at[0, part],
+                    recv_sems.at[0, part],
+                    x_peer,
+                )
+            )
+            outs[-1].start()
+        outs.append(
+            remote(buffer.at[own], buffer.at[own], send_sems.at[1, 0], recv_sems.at[1, 0], core_peer)
+        )
+        outs[-1].start()
+        return outs
+
+    def pass_on(buffer, send_sems, recv_sems, outs):
+        for part in range(2):
+            piece = pl.ds(part * half, half)
+            outs[part].wait_recv()
+            outs.append(
+                remote(
+                    buffer.at[across, piece],
+                    buffer.at[across, piece],
+                    send_sems.at[2, part],
+                    recv_sems.at[2, part],
+                    core_peer,
+                )
+            )
+            outs[-1].start()
+
+    def rows_of(block):
+        return pl.ds(pl.multiple_of(block * rows, rows), rows)
+
+    def project(block):
+        result = jnp.dot(x_all[block], qkv_w[...], preferred_element_type=jnp.float32) + qkv_b[...]
+        result = result.astype(jnp.bfloat16)
+        where = rows_of(block)
+        queries[where] = result[:, :quarter] * jnp.bfloat16(1.0 / math.sqrt(HEAD))
+        kv_out[0, where] = result[:, quarter : 2 * quarter]
+        kv_out[1, where] = result[:, 2 * quarter :]
+
+    x_copies = spread(x_all, x_s, x_r)
+    kv_step(0)
+    loads[0].wait()
+    project(own)
+    x_copies[2].wait_recv()
+    project(near_core)
+    kv_step(1)
+    pass_on(x_all, x_s, x_r, x_copies)
+    project(across)
+    for copy in x_copies[3:5]:
+        copy.wait_recv()
+    project(corner)
+    for distance in range(2, depth):
+        kv_step(distance)
+    kv_finish()
+    for load in loads[1:]:
+        load.wait()
+
+    for group in range(groups):
+        for page in range(pages):
+            slot = page_table[group, page]
+            spot = pl.ds((group * pages + page) * page_len, page_len)
+            far_k[spot] = kv_all[slot // 2, slot % 2, 0]
+            far_v[spot] = kv_all[slot // 2, slot % 2, 1]
+
+    near_len = rows * (1 + -(-(MOST_LEN - 1) // rows))
+    back = near_len // rows - 1
+    contract = (((1,), (1,)), ((), ()))
+    lane_head = lax.broadcasted_iota(jnp.int32, (1, quarter), 1) // HEAD
+
+    def attend(block):
+        first = jnp.maximum(block - back, 0) * rows
+        near = pl.ds(pl.multiple_of(first, rows), near_len)
+        query = queries[rows_of(block)]
+        place = lax.broadcasted_iota(jnp.int32, (rows, 1), 0) + block * rows
+        low = jnp.zeros((rows, 1), jnp.int32)
+        group = jnp.zeros((rows, 1), jnp.int32) + group_ids[0, 0]
+        end = lengths[0, 0]
+        for e in range(1, SEQ_DEV):
+            low = jnp.where(place >= end, end, low)
+            group = jnp.where(place >= end, group_ids[0, e], group)
+            end = end + lengths[0, e]
+        key_place = lax.broadcasted_iota(jnp.int32, (rows, near_len), 1) + first
+        allowed = (key_place >= low) & (key_place <= place)
+
+        def one_head(head, carry):
+            lanes = lane_head == head
+            mine = jnp.where(lanes, query, jnp.bfloat16(0))
+            score = lax.dot_general(
+                mine, kv_out[0, near], contract, preferred_element_type=jnp.float32
+            )
+            score = jnp.where(allowed, score, -jnp.inf)
+            top = jnp.max(score, axis=1, keepdims=True)
+            fars = []
+            for g in range(groups):
+                far = lax.dot_general(
+                    mine,
+                    far_k[pl.ds(g * far_len, far_len)],
+                    contract,
+                    preferred_element_type=jnp.float32,
+                )
+                fars.append(far)
+                best = jnp.max(far, axis=1, keepdims=True)
+                top = jnp.where(group == g, jnp.maximum(top, best), top)
+            weight = jnp.exp(score - top)
+            total = jnp.sum(weight, axis=1, keepdims=True)
+            summed = jnp.dot(
+                weight.astype(jnp.bfloat16), kv_out[1, near], preferred_element_type=jnp.float32
+            )
+            for g in range(groups):
+                weight = jnp.exp(fars[g] - jnp.where(group == g, top, FAR))
+                total = total + jnp.sum(weight, axis=1, keepdims=True)
+                summed = summed + jnp.dot(
+                    weight.astype(jnp.bfloat16),
+                    far_v[pl.ds(g * far_len, far_len)],
+                    preferred_element_type=jnp.float32,
+                )
+            attended[...] = jnp.where(lanes, summed / total, attended[...])
+            return carry
+
+        attended[...] = jnp.zeros_like(attended)
+        lax.fori_loop(0, heads, one_head, 0)
+        return jnp.dot(
+            attended[...].astype(jnp.bfloat16), out_w[...], preferred_element_type=jnp.float32
+        )
+
+    def to_core(phase, index, value):
+        part_send[phase, index] = value.astype(jnp.bfloat16)
+        copy = remote(
+            part_send.at[phase, index],
+            part_recv.at[phase, index],
+            p_s.at[phase, index],
+            p_r.at[phase, index],
+            core_peer,
+        )
+        copy.start()
+        return copy
+
+    def to_across(phase, value):
+        wide_send[phase] = value.astype(jnp.bfloat16)
+        copy = remote(
+            wide_send.at[phase], wide_recv.at[phase], p_s.at[phase, 2], p_r.at[phase, 2], x_peer
+        )
+        copy.start()
+        return copy
+
+    def norm(values, gain, bias):
+        mean = jnp.mean(values, axis=1, keepdims=True)
+        centered = values - mean
+        spread_of = jnp.mean(centered * centered, axis=1, keepdims=True)
+        return centered * lax.rsqrt(spread_of + 1e-05) * gain[...] + bias[...]
+
+    sums = [to_core(0, 0, attend(corner))]
+    value = attend(across)
+    sums[0].wait_recv()
+    sums.append(to_across(0, value + part_recv[0, 0].astype(jnp.float32)))
+    sums.append(to_core(0, 1, attend(near_core)))
+    value = attend(own) + out_b[...] + x_all[own].astype(jnp.float32)
+    sums[2].wait_recv()
+    value = value + part_recv[0, 1].astype(jnp.float32)
+    sums[1].wait_recv()
+    value = value + wide_recv[0].astype(jnp.float32)
+    n_all[own] = norm(value, gain1, bias1).astype(jnp.bfloat16)
+
+    def feed(block):
+        raised = (
+            jnp.dot(n_all[block], up_w[...], preferred_element_type=jnp.float32) + up_b[...]
+        )
+        inner = raised * (1.0 + lax.erf(raised * (1.0 / math.sqrt(2.0)))) * 0.5
+        return jnp.dot(
+            inner.astype(jnp.bfloat16), down_w[...], preferred_element_type=jnp.float32
+        )
+
+    n_copies = spread(n_all, n_s, n_r)
+    kept[0] = feed(own) + down_b[...] + n_all[own].astype(jnp.float32)
+    n_copies[2].wait_recv()
+    sums.append(to_core(1, 1, feed(near_core)))
+    pass_on(n_all, n_s, n_r, n_copies)
+    kept[1] = feed(across)
+    for copy in n_copies[3:5]:
+        copy.wait_recv()
+    sums.append(to_core(1, 0, feed(corner)))
+    sums[4].wait_recv()
+    sums.append(to_across(1, kept[1] + part_recv[1, 0].astype(jnp.float32)))
+    sums[3].wait_recv()
+    value = kept[0] + part_recv[1, 1].astype(jnp.float32)
+    sums[5].wait_recv()
+    value = value + wide_recv[1].astype(jnp.float32)
+    hidden[...] = norm(value, gain2, bias2).astype(jnp.bfloat16)
+    for copy in deals + x_copies + n_copies + sums:
+        copy.wait_send()
+
+
+def kernel_local(
+    tokens,
+    deal,
+    lengths,
+    group_ids,
+    page_table,
+    prefix_cache,
+    qkv_weight,
+    qkv_bias,
+    out_weight,
+    out_bias,
+    norm1_gain,
+    norm1_bias,
+    up_weight,
+    up_bias,
+    down_weight,
+    down_bias,
+    norm2_gain,
+    norm2_bias,
+):
+    n_tok = lax.axis_size("tok")
+    rows, width = tokens.shape
+    quarter = qkv_weight.shape[2]
+    hidden_dev = up_weight.shape[1]
+    slots, page_len = prefix_cache.shape[:2]
+    groups, pages = page_table.shape
+    far_keys = groups * pages * page_len
+    block_rows = 4 * rows
+    vmem = pl.BlockSpec(memory_space=pltpu.VMEM)
+    smem = pl.BlockSpec(memory_space=pltpu.SMEM)
+    anywhere = pl.BlockSpec(memory_space=pl.ANY)
+    dma = pltpu.SemaphoreType.DMA
+    half = jnp.bfloat16
+    hidden, kv_out = pl.pallas_call(
+        functools.partial(layer_kernel, n_tok),
+        out_shape=(
+            jax.ShapeDtypeStruct((rows, width), half),
+            jax.ShapeDtypeStruct((2, block_rows, quarter), half),
+        ),
+        in_specs=[
+            vmem, vmem, smem, smem, smem, vmem, anywhere, vmem, anywhere,
+            vmem, vmem, vmem, anywhere, vmem, anywhere, vmem, vmem, vmem,
+        ],
+        out_specs=(vmem, vmem),
+        scratch_shapes=[
+            pltpu.VMEM((width, 3 * quarter), half),
+            pltpu.VMEM((quarter, width), half),
+            pltpu.VMEM((width, hidden_dev), half),
+            pltpu.VMEM((hidden_dev, width), half),
+            pltpu.VMEM((rows, width), half),
+            pltpu.VMEM((4, rows, width), half),
+            pltpu.VMEM((n_tok, slots, 2, page_len, quarter), half),
+            pltpu.VMEM((far_keys, quarter), half),
+            pltpu.VMEM((far_keys, quarter), half),
+            pltpu.VMEM((block_rows, quarter), half),
+            pltpu.VMEM((rows, quarter), jnp.float32),
+            pltpu.VMEM((2, 2, rows, width), half),
+            pltpu.VMEM((2, 2, rows, width), half),
+            pltpu.VMEM((2, rows, width), half),
+            pltpu.VMEM((2, rows, width), half),
+            pltpu.VMEM((4, rows, width), half),
+            pltpu.VMEM((2, rows, width), jnp.float32),
+            dma((4,)),
+            dma((n_tok,)),
+            dma((n_tok,)),
+            dma((n_tok, slots, 3)),
+            dma((n_tok, slots)),
+            dma((3, 2)),
+            dma((3, 2)),
+            dma((2, 3)),
+            dma((2, 3)),
+            dma((3, 2)),
+            dma((3, 2)),
+        ],
+        compiler_params=pltpu.CompilerParams(
+            collective_id=0, has_side_effects=True, vmem_limit_bytes=56 * 2**20
+        ),
+    )(
+        tokens,
+        deal.reshape(1, rows),
+        lengths,
+        group_ids,
+        page_table,
+        prefix_cache.transpose(0, 2, 1, 3),
+        qkv_weight.reshape(width, 3 * quarter),
+        qkv_bias.reshape(1, 3 * quarter),
+        out_weight,
+        out_bias.reshape(1, width),
+        norm1_gain.reshape(1, width),
+        norm1_bias.reshape(1, width),
+        up_weight,
+        up_bias.reshape(1, hidden_dev),
+        down_weight,
+        down_bias.reshape(1, width),
+        norm2_gain.reshape(1, width),
+        norm2_bias.reshape(1, width),
+    )
+    return (hidden, kv_out.transpose(1, 0, 2))
+
+
 def solution(mesh):
+    tok_count = mesh.shape["tok"]
+    fits = tok_count <= 8 and mesh.shape["wa"] == 2 and mesh.shape["wb"] == 2
     return jax.shard_map(
-        local,
+        kernel_local if fits else collective_local,
         mesh=mesh,
         in_specs=(
             P(("tok", "wa", "wb"), None),

time: 212 us -> 82.6 us (0.39)
  waiting for transfers between devices: 122 us -> 0 us
  Pallas kernels: 0 us -> 73 us
  matrix products: 24 us -> 0 us
  other arithmetic: 16.9 us -> 0 us
  local copies, waits for them, and re-layouts: 24.1 us -> 8.67 us
  between operations: 14.6 us -> 0.66 us
  starting transfers between devices: 7.85 us -> 0 us
    pallas_call x0 -> x1, Pallas kernels: none -> 73 us  [kernel_local(): pl.pallas_call(functools.partial(layer_kernel, n_tok), out_shape=(jax.Sha...]
    all_gather x3 -> x0, waiting for transfers between devices: 68.1 us -> none  [the longest x1 42.3 us: local(): piece = lax.all_gather(prefix_cache, 'tok', axis=0, tiled=True)]
    reduce_scatter x2 -> x0, waiting for transfers between devices: 45.7 us -> none  [narrow(): lax.psum_scatter(jnp.dot(values, weight, preferred_element_type=jnp.float...]
    dot_general x7 -> x0, matrix products: 24 us -> none  [the longest x2 11.7 us: narrow(): jnp.dot(values, weight, preferred_element_type=jnp.float32)]
    gather x5 -> x0, local copies, waits for them, and re-layouts: 9.49 us -> none  [the longest x3 7.97 us: compute(): jnp.take(piece, picks, axis=0).reshape(step * page_len, 2, heads_dev, HEAD)]
    reduce_sum x11 -> x0, other arithmetic: 8.32 us -> none  [the longest x2 2.37 us: layer_norm(): spread = jnp.mean(centered * centered, axis=-1, keepdims=True)]
    all_to_all x1 -> x0, waiting for transfers between devices: 8.18 us -> none  [local(): lax.all_to_all(tokens.reshape(tok_count, run_len, width), 'tok', split_ax...]
    all_to_all x1 -> x0, starting transfers between devices: 7.42 us -> none  [local(): lax.all_to_all(tokens.reshape(tok_count, run_len, width), 'tok', split_ax...]
  transfers between devices with their start and end apart: 6 -> 0, of which waited for: 6 -> 0; matrix products, arithmetic and copies ran while one was open for 9% -> 0% of each run, Pallas kernels for 0% -> 0%
where the time goes in v1:
time: 82.6 us; the launch traced here: 82.3 us
  Pallas kernels  73 us (88%)
  local copies, waits for them, and re-layouts  8.67 us (10%)
    pallas_call x1, Pallas kernels, kernel_local(): pl.pallas_call(functools.partial(layer_kernel, n_tok), out_shape=(jax.Sha...  73 us
    unnamed x9, local copies, waits for them, and re-layouts  7.08 us

profile of v1, /device:TPU:0, one launch (start us, length us, event | category | flops | bytes accessed | tf_op | source)
XLA Modules:
  0.0 82.3 jit_solution(18150115787195869661)
XLA Ops:
  0.6 1.7 %copy.24 = bf16[1024,3,256]{0,2,1:T(8,128)(2,1)S(1)} copy(bf16[1024,3,256]{2,0,1:T(8,128)(2,1)} %param.24) | data formatting | bytes 3145728 | tf_op args[6]
  2.4 0.0 copy-start
  2.4 0.0 copy-start.1
  2.4 1.6 %copy.25.qkv_w_hbm = bf16[1024,768]{1,0:T(8,128)(2,1)} copy(bf16[1024,768]{0,1:T(8,128)(2,1)S(1)} %bitcast.16) | data formatting | bytes 3145728 | tf_op jit(solution)/shard_map/reshape | solution.py:655
  4.0 0.0 copy-done
  4.0 0.7 copy.29
  4.7 0.0 copy-done.1
  4.7 0.6 copy.27
  5.3 73.0 %shard_map.185 = (bf16[128,1024]{1,0:T(8,128)(2,1)}, bf16[2,512,256]{2,1,0:T(8,128)(2,1)}) custom-call(bf16[128,1024]{1,0:T(8,128)(2,1)} %tokens.1, s32[1,128]{1,0:T(1,128)} %bitcast.28, s32[1,8]{1,0:T(1,128)} %lengths.1, s32[1,8]{1,0:T(1,128)} %group_ids.1, s32[2,4]{1,0:T(2,128)} %page_table.1, bf16[2,2,128,256]{3,2,1,0:T(8,128)(2,1)} %bitcast.17, ...), custom_call_target="tpu_custom_call" | custom-call | tf_op jit(solution)/shard_map/pallas_call | solution.py:604
  78.3 2.4 %copy.26 = bf16[512,2,256]{2,1,0:T(2,128)(2,1)} copy(bf16[512,2,256]{2,0,1:T(8,128)(2,1)} %bitcast.18) | data formatting | bytes 1048576
  80.7 1.7 %copy.31 = bf16[128,1024]{1,0:T(8,128)(2,1)} copy(bf16[128,1024]{1,0:T(8,128)(2,1)} %get-tuple-element.12) | data formatting | bytes 524288
Async XLA Ops:
  2.4 1.6 %copy-start = (bf16[2,128,2,256]{3,2,1,0:T(2,128)(2,1)S(1)}, bf16[2,128,2,256]{3,2,1,0:T(2,128)(2,1)}, u32[]{:S(2)}) copy-start(bf16[2,128,2,256]{3,2,1,0:T(2,128)(2,1)} %param.23) | copy-start | bytes 786436
  2.4 2.3 %copy-start.1 = (f32[3,256]{1,0:T(4,128)S(1)}, f32[3,256]{1,0:T(4,128)}, u32[]{:S(2)}) copy-start(f32[3,256]{1,0:T(4,128)} %param.25) | copy-start | bytes 9220

commit v2 on v1

--- a/solution.py
+++ b/solution.py
@@ -11,6 +11,7 @@
 HEAD = 64
 SEQ_DEV = 8
 MOST_LEN = 192
+PARTS = 2
 FAR = 3e38
 MESH = pl.DeviceIdType.MESH
 
@@ -186,7 +187,7 @@
     gain2,
     bias2,
     hidden,
-    kv_out,
+    kv_out_hbm,
     qkv_w,
     out_w,
     up_w,
@@ -194,6 +195,7 @@
     arrived,
     x_all,
     kv_all,
+    kv_out,
     far_k,
     far_v,
     queries,
@@ -221,7 +223,7 @@
     b = lax.axis_index("wb")
     rows, width = tokens.shape
     run = rows // n_tok
-    quarter = qkv_b.shape[1] // 3
+    quarter = qkv_b.shape[1]
     heads = quarter // HEAD
     groups, pages = page_table.shape
     page_len = own_kv.shape[2]
@@ -235,15 +237,21 @@
     core_peer = (tok, a, 1 - b)
     x_peer = (tok, 1 - a, b)
 
+    def run_at(index):
+        return pl.ds(pl.multiple_of(index * run, run), run)
+
+    pairs = (
+        (tokens.at[run_at(tok)], arrived.at[run_at(tok)]),
+        (qkv_w_hbm, qkv_w),
+        (out_w_hbm, out_w),
+        (up_w_hbm, up_w),
+        (down_w_hbm, down_w),
+        (own_kv, kv_all.at[tok]),
+    )
     loads = [
         pltpu.make_async_copy(src, dst, w_sem.at[i])
-        for i, (src, dst) in enumerate(
-            ((qkv_w_hbm, qkv_w), (out_w_hbm, out_w), (up_w_hbm, up_w), (down_w_hbm, down_w))
-        )
+        for i, (src, dst) in enumerate(pairs)
     ]
-    for load in loads:
-        load.start()
-
     barrier = pltpu.get_barrier_semaphore()
     for d in range(1, n_tok):
         pl.semaphore_signal(
@@ -251,6 +259,8 @@
         )
     for peer in (core_peer, x_peer):
         pl.semaphore_signal(barrier, inc=1, device_id=peer, device_id_type=MESH)
+    for load in loads[:1]:
+        load.start()
     pl.semaphore_wait(barrier, n_tok + 1)
 
     def remote(src, dst, send_sem, recv_sem, peer):
@@ -263,9 +273,6 @@
             device_id_type=MESH,
         )
 
-    def run_at(index):
-        return pl.ds(pl.multiple_of(index * run, run), run)
-
     deals = []
     for d in range(1, n_tok):
         to = lax.rem(tok + d, n_tok)
@@ -312,47 +319,49 @@
     def kv_arrived(source, slot):
         kv_copy(source, slot, PAIR, False).wait_recv()
 
-    other = z * 2 + (1 - y)
-    kv_each(tok, 1, (PAIR,), begin, True)
-    kv_each(tok, 0, (RIGHT, LEFT), begin, True)
-    kv_each(tok, 1, (RIGHT, LEFT), begin, True)
-    kv_each(tok, 0, (PAIR,), begin, True)
-    kv_all[tok] = own_kv[...]
-
-    def kv_step(distance):
-        if distance == 0:
-            kv_arrived(other, 1)
-            kv_each(other, 1, (RIGHT, LEFT), begin)
-            return
+    for slot in range(2):
+        kv_each(tok, slot, (RIGHT, LEFT, PAIR), begin, True)
+    for load in loads[1:]:
+        load.start()
+
+    def kv_along(distance, action):
         for way, base in ((RIGHT, z - distance), (LEFT, z + distance)):
 
             @pl.when((base >= 0) & (base < depth))
             def _():
-                same, cross = base * 2 + y, base * 2 + (1 - y)
-                kv_arrived(same, 0)
-                kv_each(same, 0, (way, PAIR), begin)
-                kv_arrived(same, 1)
-                kv_each(same, 1, (way,), begin)
-                kv_arrived(cross, 1)
-                kv_each(cross, 1, (way,), begin)
+                action(base * 2 + y, way)
+
+    def kv_step(distance, slot):
+        def onward(source, way):
+            kv_arrived(source, slot)
+            kv_each(source, slot, (way, PAIR), begin)
+
+        if distance < depth:
+            kv_along(distance, onward)
 
     def kv_finish():
-        for base in range(depth):
-            kv_arrived(base * 2 + (1 - y), 0)
-        kv_each(tok, 0, (RIGHT, LEFT, PAIR), sent, True)
-        kv_each(tok, 1, (RIGHT, LEFT, PAIR), sent, True)
-        kv_each(other, 1, (RIGHT, LEFT), sent)
+        for distance in range(depth):
+
+            def wait_pair(source, way):
+                for slot in range(2):
+                    kv_arrived(source + 1 - 2 * y, slot)
+
+            if distance == 0:
+                wait_pair(tok, PAIR)
+            else:
+                kv_along(distance, wait_pair)
+
+    def kv_drain():
+        for slot in range(2):
+            kv_each(tok, slot, (RIGHT, LEFT, PAIR), sent, True)
         for distance in range(1, depth):
-            for way, base in ((RIGHT, z - distance), (LEFT, z + distance)):
-
-                @pl.when((base >= 0) & (base < depth))
-                def _():
-                    same, cross = base * 2 + y, base * 2 + (1 - y)
-                    kv_each(same, 0, (way, PAIR), sent)
-                    kv_each(same, 1, (way,), sent)
-                    kv_each(cross, 1, (way,), sent)
-
-    arrived[run_at(tok)] = tokens[run_at(tok)]
+
+            def drain(source, way):
+                for slot in range(2):
+                    kv_each(source, slot, (way, PAIR), sent)
+
+            kv_along(distance, drain)
+
     places = deal[...]
     source = places // (4 * rows) * run + lax.rem(places, run)
     hot = jnp.where(
@@ -361,77 +370,71 @@
         0.0,
     )
     pick = hot.T.astype(jnp.bfloat16)
+    loads[0].wait()
     for copy in deals:
         copy.wait_recv()
     x_all[own] = jnp.dot(pick, arrived[...], preferred_element_type=jnp.float32).astype(
         jnp.bfloat16
     )
 
-    half = rows // 2
-
-    def spread(buffer, send_sems, recv_sems):
-        outs = []
-        for part in range(2):
-            piece = pl.ds(part * half, half)
-            outs.append(
-                remote(
-                    buffer.at[own, piece],
-                    buffer.at[own, piece],
-                    send_sems.at[0, part],
-                    recv_sems.at[0, part],
-                    x_peer,
-                )
-            )
-            outs[-1].start()
-        outs.append(
-            remote(buffer.at[own], buffer.at[own], send_sems.at[1, 0], recv_sems.at[1, 0], core_peer)
-        )
-        outs[-1].start()
-        return outs
-
-    def pass_on(buffer, send_sems, recv_sems, outs):
-        for part in range(2):
-            piece = pl.ds(part * half, half)
-            outs[part].wait_recv()
-            outs.append(
-                remote(
-                    buffer.at[across, piece],
-                    buffer.at[across, piece],
-                    send_sems.at[2, part],
-                    recv_sems.at[2, part],
-                    core_peer,
-                )
-            )
-            outs[-1].start()
+    half = rows // PARTS
+
+    def piece(part):
+        return pl.ds(part * half, half)
+
+    def rows_to(buffer, block, part, way, send_sems, recv_sems, peer):
+        copy = remote(
+            buffer.at[block, piece(part)],
+            buffer.at[block, piece(part)],
+            send_sems.at[way, part],
+            recv_sems.at[way, part],
+            peer,
+        )
+        copy.start()
+        return copy
 
     def rows_of(block):
         return pl.ds(pl.multiple_of(block * rows, rows), rows)
 
     def project(block):
-        result = jnp.dot(x_all[block], qkv_w[...], preferred_element_type=jnp.float32) + qkv_b[...]
-        result = result.astype(jnp.bfloat16)
         where = rows_of(block)
-        queries[where] = result[:, :quarter] * jnp.bfloat16(1.0 / math.sqrt(HEAD))
-        kv_out[0, where] = result[:, quarter : 2 * quarter]
-        kv_out[1, where] = result[:, 2 * quarter :]
-
-    x_copies = spread(x_all, x_s, x_r)
-    kv_step(0)
-    loads[0].wait()
+        states = x_all[block]
+        for part in range(3):
+            result = jnp.dot(states, qkv_w[part], preferred_element_type=jnp.float32)
+            result = (result + qkv_b[part : part + 1]).astype(jnp.bfloat16)
+            if part == 0:
+                queries[where] = result * jnp.bfloat16(1.0 / math.sqrt(HEAD))
+            else:
+                kv_out[part - 1, where] = result
+
+    x_in = [rows_to(x_all, own, part, 0, x_s, x_r, x_peer) for part in range(PARTS)]
+    x_core = [rows_to(x_all, own, part, 1, x_s, x_r, core_peer) for part in range(PARTS)]
+    x_pass = []
+    kv_step(1, 0)
+    loads[1].wait()
     project(own)
-    x_copies[2].wait_recv()
+    kv_step(1, 1)
+    for copy in x_core:
+        copy.wait_recv()
     project(near_core)
-    kv_step(1)
-    pass_on(x_all, x_s, x_r, x_copies)
+    for part in range(PARTS):
+        x_in[part].wait_recv()
+        x_pass.append(rows_to(x_all, across, part, 2, x_s, x_r, core_peer))
+        if part == 0:
+            kv_step(2, 0)
     project(across)
-    for copy in x_copies[3:5]:
+    kv_step(2, 1)
+    for copy in x_pass:
         copy.wait_recv()
     project(corner)
-    for distance in range(2, depth):
-        kv_step(distance)
+    cache_out = pltpu.make_async_copy(kv_out, kv_out_hbm, w_sem.at[6])
+    cache_out.start()
+    for distance in range(3, depth):
+        for slot in range(2):
+            kv_step(distance, slot)
+    for load in loads[2:]:
+        load.wait()
     kv_finish()
-    for load in loads[1:]:
-        load.wait()
 
     for group in range(groups):
         for page in range(pages):
@@ -501,25 +504,31 @@
             attended[...].astype(jnp.bfloat16), out_w[...], preferred_element_type=jnp.float32
         )
 
-    def to_core(phase, index, value):
-        part_send[phase, index] = value.astype(jnp.bfloat16)
+    def to_core(phase, index, part, value):
+        where = (phase, index) if part is None else (phase, index, piece(part))
+        sem = (phase, index, part or 0)
+        part_send[where] = value.astype(jnp.bfloat16)
         copy = remote(
-            part_send.at[phase, index],
-            part_recv.at[phase, index],
-            p_s.at[phase, index],
-            p_r.at[phase, index],
-            core_peer,
+            part_send.at[where], part_recv.at[where], p_s.at[sem], p_r.at[sem], core_peer
         )
         copy.start()
         return copy
 
-    def to_across(phase, value):
-        wide_send[phase] = value.astype(jnp.bfloat16)
+    def to_across(phase, part, value):
+        where = (phase, piece(part))
+        wide_send[where] = value.astype(jnp.bfloat16)
         copy = remote(
-            wide_send.at[phase], wide_recv.at[phase], p_s.at[phase, 2], p_r.at[phase, 2], x_peer
+            wide_send.at[where],
+            wide_recv.at[where],
+            p_s.at[phase, 2, part],
+            p_r.at[phase, 2, part],
+            x_peer,
         )
         copy.start()
         return copy
+
+    def got(ref, *where):
+        return ref[where].astype(jnp.float32)
 
     def norm(values, gain, bias):
         mean = jnp.mean(values, axis=1, keepdims=True)
@@ -527,45 +536,60 @@
         spread_of = jnp.mean(centered * centered, axis=1, keepdims=True)
         return centered * lax.rsqrt(spread_of + 1e-05) * gain[...] + bias[...]
 
-    sums = [to_core(0, 0, attend(corner))]
-    value = attend(across)
-    sums[0].wait_recv()
-    sums.append(to_across(0, value + part_recv[0, 0].astype(jnp.float32)))
-    sums.append(to_core(0, 1, attend(near_core)))
-    value = attend(own) + out_b[...] + x_all[own].astype(jnp.float32)
-    sums[2].wait_recv()
-    value = value + part_recv[0, 1].astype(jnp.float32)
-    sums[1].wait_recv()
-    value = value + wide_recv[0].astype(jnp.float32)
-    n_all[own] = norm(value, gain1, bias1).astype(jnp.bfloat16)
-
-    def feed(block):
-        raised = (
-            jnp.dot(n_all[block], up_w[...], preferred_element_type=jnp.float32) + up_b[...]
-        )
+    corner_copy = to_core(0, 0, None, attend(corner))
+    kept[1] = attend(across)
+    corner_copy.wait_recv()
+    wide = [
+        to_across(0, part, kept[1, piece(part)] + got(part_recv, 0, 0, piece(part)))
+        for part in range(PARTS)
+    ]
+    core_copy = to_core(0, 1, None, attend(near_core))
+    kept[0] = attend(own) + out_b[...] + got(x_all, own)
+    core_copy.wait_recv()
+    sums = [corner_copy, core_copy] + wide
+    n_in, n_core, n_pass = [], [], []
+    for part in range(PARTS):
+        value = kept[0, piece(part)] + got(part_recv, 0, 1, piece(part))
+        wide[part].wait_recv()
+        value = value + got(wide_recv, 0, piece(part))
+        n_all[own, piece(part)] = norm(value, gain1, bias1).astype(jnp.bfloat16)
+        n_in.append(rows_to(n_all, own, part, 0, n_s, n_r, x_peer))
+        n_core.append(rows_to(n_all, own, part, 1, n_s, n_r, core_peer))
+
+    def feed(states):
+        raised = jnp.dot(states, up_w[...], preferred_element_type=jnp.float32) + up_b[...]
         inner = raised * (1.0 + lax.erf(raised * (1.0 / math.sqrt(2.0)))) * 0.5
         return jnp.dot(
             inner.astype(jnp.bfloat16), down_w[...], preferred_element_type=jnp.float32
         )
 
-    n_copies = spread(n_all, n_s, n_r)
-    kept[0] = feed(own) + down_b[...] + n_all[own].astype(jnp.float32)
-    n_copies[2].wait_recv()
-    sums.append(to_core(1, 1, feed(near_core)))
-    pass_on(n_all, n_s, n_r, n_copies)
-    kept[1] = feed(across)
-    for copy in n_copies[3:5]:
+    kept[0] = feed(n_all[own]) + down_b[...] + got(n_all, own)
+    for copy in n_core:
         copy.wait_recv()
-    sums.append(to_core(1, 0, feed(corner)))
-    sums[4].wait_recv()
-    sums.append(to_across(1, kept[1] + part_recv[1, 0].astype(jnp.float32)))
-    sums[3].wait_recv()
-    value = kept[0] + part_recv[1, 1].astype(jnp.float32)
-    sums[5].wait_recv()
-    value = value + wide_recv[1].astype(jnp.float32)
-    hidden[...] = norm(value, gain2, bias2).astype(jnp.bfloat16)
-    for copy in deals + x_copies + n_copies + sums:
+    core_copy = to_core(1, 1, None, feed(n_all[near_core]))
+    sums.append(core_copy)
+    wide = []
+    for part in range(PARTS):
+        n_in[part].wait_recv()
+        n_pass.append(rows_to(n_all, across, part, 2, n_s, n_r, core_peer))
+        kept[1, piece(part)] = feed(n_all[across, piece(part)])
+        n_pass[part].wait_recv()
+        corner_copy = to_core(1, 0, part, feed(n_all[corner, piece(part)]))
+        sums.append(corner_copy)
+        corner_copy.wait_recv()
+        wide.append(
+            to_across(1, part, kept[1, piece(part)] + got(part_recv, 1, 0, piece(part)))
+        )
+    core_copy.wait_recv()
+    for part in range(PARTS):
+        value = kept[0, piece(part)] + got(part_recv, 1, 1, piece(part))
+        wide[part].wait_recv()
+        value = value + got(wide_recv, 1, piece(part))
+        hidden[piece(part)] = norm(value, gain2, bias2).astype(jnp.bfloat16)
+    for copy in deals + x_in + x_core + x_pass + n_in + n_core + n_pass + sums + wide:
         copy.wait_send()
+    kv_drain()
+    cache_out.wait()
 
 
 def kernel_local(
@@ -608,18 +632,19 @@
             jax.ShapeDtypeStruct((2, block_rows, quarter), half),
         ),
         in_specs=[
-            vmem, vmem, smem, smem, smem, vmem, anywhere, vmem, anywhere,
+            anywhere, vmem, smem, smem, smem, anywhere, anywhere, vmem, anywhere,
             vmem, vmem, vmem, anywhere, vmem, anywhere, vmem, vmem, vmem,
         ],
-        out_specs=(vmem, vmem),
+        out_specs=(vmem, anywhere),
         scratch_shapes=[
-            pltpu.VMEM((width, 3 * quarter), half),
+            pltpu.VMEM((3, width, quarter), half),
             pltpu.VMEM((quarter, width), half),
             pltpu.VMEM((width, hidden_dev), half),
             pltpu.VMEM((hidden_dev, width), half),
             pltpu.VMEM((rows, width), half),
             pltpu.VMEM((4, rows, width), half),
             pltpu.VMEM((n_tok, slots, 2, page_len, quarter), half),
+            pltpu.VMEM((2, block_rows, quarter), half),
             pltpu.VMEM((far_keys, quarter), half),
             pltpu.VMEM((far_keys, quarter), half),
             pltpu.VMEM((block_rows, quarter), half),
@@ -630,17 +655,17 @@
             pltpu.VMEM((2, rows, width), half),
             pltpu.VMEM((4, rows, width), half),
             pltpu.VMEM((2, rows, width), jnp.float32),
-            dma((4,)),
+            dma((7,)),
             dma((n_tok,)),
             dma((n_tok,)),
             dma((n_tok, slots, 3)),
             dma((n_tok, slots)),
-            dma((3, 2)),
-            dma((3, 2)),
-            dma((2, 3)),
-            dma((2, 3)),
-            dma((3, 2)),
-            dma((3, 2)),
+            dma((3, PARTS)),
+            dma((3, PARTS)),
+            dma((2, 3, PARTS)),
+            dma((2, 3, PARTS)),
+            dma((3, PARTS)),
+            dma((3, PARTS)),
         ],
         compiler_params=pltpu.CompilerParams(
             collective_id=0, has_side_effects=True, vmem_limit_bytes=56 * 2**20
@@ -652,8 +677,8 @@
         group_ids,
         page_table,
         prefix_cache.transpose(0, 2, 1, 3),
-        qkv_weight.reshape(width, 3 * quarter),
-        qkv_bias.reshape(1, 3 * quarter),
+        qkv_weight.transpose(1, 0, 2),
+        qkv_bias,
         out_weight,
         out_bias.reshape(1, width),
         norm1_gain.reshape(1, width),

time: 82.6 us -> 73 us (0.88)
  Pallas kernels: 73 us -> 66.4 us
  local copies, waits for them, and re-layouts: 8.67 us -> 5.72 us
    pallas_call x1, Pallas kernels: 73 us -> 66.4 us  [kernel_local(): pl.pallas_call(functools.partial(layer_kernel, n_tok), out_shape=(jax.Sha...]
    reshape x1 -> x0, local copies, waits for them, and re-layouts: 1.59 us -> none  [kernel_local(): qkv_weight.reshape(width, 3 * quarter)]
    unnamed x9 -> x3, local copies, waits for them, and re-layouts: 7.08 us -> 5.72 us
where the time goes in v2:
time: 73 us; the launch traced here: 72.7 us
  Pallas kernels  66.4 us (91%)
  local copies, waits for them, and re-layouts  5.72 us (8%)
    pallas_call x1, Pallas kernels, kernel_local(): pl.pallas_call(functools.partial(layer_kernel, n_tok), out_shape=(jax.Sha...  66.4 us
    unnamed x3, local copies, waits for them, and re-layouts  5.72 us

profile of v2, /device:TPU:0, one launch (start us, length us, event | category | flops | bytes accessed | tf_op | source)
XLA Modules:
  0.0 72.7 jit_solution(16475935843085031737)
XLA Ops:
  0.6 1.7 %copy.23 = bf16[2,128,2,256]{3,1,2,0:T(8,128)(2,1)} copy(bf16[2,128,2,256]{3,2,1,0:T(2,128)(2,1)} %param.23) | data formatting | bytes 524288 | tf_op args[5]
  2.3 66.4 %shard_map.185 = (bf16[128,1024]{1,0:T(8,128)(2,1)}, bf16[2,512,256]{2,1,0:T(8,128)(2,1)}) custom-call(bf16[128,1024]{1,0:T(8,128)(2,1)} %tokens.1, s32[1,128]{1,0:T(1,128)} %bitcast.23, s32[1,8]{1,0:T(1,128)} %lengths.1, s32[1,8]{1,0:T(1,128)} %group_ids.1, s32[2,4]{1,0:T(2,128)} %page_table.1, bf16[2,2,128,256]{3,2,1,0:T(8,128)(2,1)} %bitcast.14, ...), custom_call_target="tpu_custom_call" | custom-call | tf_op jit(solution)/shard_map/pallas_call | solution.py:628
  68.7 2.4 %copy.21 = bf16[512,2,256]{2,1,0:T(2,128)(2,1)} copy(bf16[512,2,256]{2,0,1:T(8,128)(2,1)} %bitcast.15) | data formatting | bytes 1048576
  71.1 1.7 %copy.25 = bf16[128,1024]{1,0:T(8,128)(2,1)} copy(bf16[128,1024]{1,0:T(8,128)(2,1)} %get-tuple-element.10) | data formatting | bytes 524288

commit v3 on v2

--- a/solution.py
+++ b/solution.py
@@ -196,10 +196,16 @@
     x_all,
     kv_all,
     kv_out,
+    kv_pair,
     far_k,
     far_v,
     queries,
-    attended,
+    near_sum,
+    near_top,
+    near_total,
+    far_sum,
+    far_top,
+    far_total,
     part_send,
     part_recv,
     wide_send,
@@ -406,6 +412,7 @@
                 queries[where] = result * jnp.bfloat16(1.0 / math.sqrt(HEAD))
             else:
                 kv_out[part - 1, where] = result
+        kv_pair[where] = jnp.stack([kv_out[0, where], kv_out[1, where]], axis=1)
 
     x_in = [rows_to(x_all, own, part, 0, x_s, x_r, x_peer) for part in range(PARTS)]
     x_core = [rows_to(x_all, own, part, 1, x_s, x_r, core_peer) for part in range(PARTS)]
@@ -427,38 +434,26 @@
     for copy in x_pass:
         copy.wait_recv()
     project(corner)
-    cache_out = pltpu.make_async_copy(kv_out, kv_out_hbm, w_sem.at[6])
+    cache_out = pltpu.make_async_copy(kv_pair, kv_out_hbm, w_sem.at[6])
     cache_out.start()
-    for distance in range(3, depth):
-        for slot in range(2):
-            kv_step(distance, slot)
-    for load in loads[2:]:
-        load.wait()
-    kv_finish()
-
-    for group in range(groups):
-        for page in range(pages):
-            slot = page_table[group, page]
-            spot = pl.ds((group * pages + page) * page_len, page_len)
-            far_k[spot] = kv_all[slot // 2, slot % 2, 0]
-            far_v[spot] = kv_all[slot // 2, slot % 2, 1]
-
     near_len = rows * (1 + -(-(MOST_LEN - 1) // rows))
     back = near_len // rows - 1
     contract = (((1,), (1,)), ((), ()))
     lane_head = lax.broadcasted_iota(jnp.int32, (1, quarter), 1) // HEAD
 
-    def attend(block):
+    def put(ref, where, lanes, value):
+        ref[where] = jnp.where(lanes, value, ref[where])
+
+    def attend_near(block):
         first = jnp.maximum(block - back, 0) * rows
         near = pl.ds(pl.multiple_of(first, rows), near_len)
-        query = queries[rows_of(block)]
+        where = rows_of(block)
+        query = queries[where]
         place = lax.broadcasted_iota(jnp.int32, (rows, 1), 0) + block * rows
         low = jnp.zeros((rows, 1), jnp.int32)
-        group = jnp.zeros((rows, 1), jnp.int32) + group_ids[0, 0]
         end = lengths[0, 0]
         for e in range(1, SEQ_DEV):
             low = jnp.where(place >= end, end, low)
-            group = jnp.where(place >= end, group_ids[0, e], group)
             end = end + lengths[0, e]
         key_place = lax.broadcasted_iota(jnp.int32, (rows, near_len), 1) + first
         allowed = (key_place >= low) & (key_place <= place)
@@ -471,7 +466,32 @@
             )
             score = jnp.where(allowed, score, -jnp.inf)
             top = jnp.max(score, axis=1, keepdims=True)
+            weight = jnp.exp(score - top)
+            summed = jnp.dot(
+                weight.astype(jnp.bfloat16), kv_out[1, near], preferred_element_type=jnp.float32
+            )
+            put(near_top, where, lanes, top)
+            put(near_total, where, lanes, jnp.sum(weight, axis=1, keepdims=True))
+            put(near_sum, where, lanes, summed)
+            return carry
+
+        lax.fori_loop(0, heads, one_head, 0)
+
+    def attend(block):
+        where = rows_of(block)
+        query = queries[where]
+        place = lax.broadcasted_iota(jnp.int32, (rows, 1), 0) + block * rows
+        group = jnp.zeros((rows, 1), jnp.int32) + group_ids[0, 0]
+        end = lengths[0, 0]
+        for e in range(1, SEQ_DEV):
+            group = jnp.where(place >= end, group_ids[0, e], group)
+            end = end + lengths[0, e]
+
+        def one_head(head, carry):
+            lanes = lane_head == head
+            mine = jnp.where(lanes, query, jnp.bfloat16(0))
             fars = []
+            top = jnp.full((rows, 1), -jnp.inf, jnp.float32)
             for g in range(groups):
                 far = lax.dot_general(
                     mine,
@@ -480,13 +500,9 @@
                     preferred_element_type=jnp.float32,
                 )
                 fars.append(far)
-                best = jnp.max(far, axis=1, keepdims=True)
-                top = jnp.where(group == g, jnp.maximum(top, best), top)
-            weight = jnp.exp(score - top)
-            total = jnp.sum(weight, axis=1, keepdims=True)
-            summed = jnp.dot(
-                weight.astype(jnp.bfloat16), kv_out[1, near], preferred_element_type=jnp.float32
-            )
+                top = jnp.where(group == g, jnp.max(far, axis=1, keepdims=True), top)
+            total = jnp.zeros((rows, 1), jnp.float32)
+            summed = jnp.zeros((rows, quarter), jnp.float32)
             for g in range(groups):
                 weight = jnp.exp(fars[g] - jnp.where(group == g, top, FAR))
                 total = total + jnp.sum(weight, axis=1, keepdims=True)
@@ -495,14 +511,40 @@
                     far_v[pl.ds(g * far_len, far_len)],
                     preferred_element_type=jnp.float32,
                 )
-            attended[...] = jnp.where(lanes, summed / total, attended[...])
+            put(far_top, ..., lanes, top)
+            put(far_total, ..., lanes, total)
+            put(far_sum, ..., lanes, summed)
             return carry
 
-        attended[...] = jnp.zeros_like(attended)
         lax.fori_loop(0, heads, one_head, 0)
-        return jnp.dot(
-            attended[...].astype(jnp.bfloat16), out_w[...], preferred_element_type=jnp.float32
-        )
+        top = jnp.maximum(near_top[where], far_top[...])
+        near_share = jnp.exp(near_top[where] - top)
+        far_share = jnp.exp(far_top[...] - top)
+        total = near_total[where] * near_share + far_total[...] * far_share
+        attended = (near_sum[where] * near_share + far_sum[...] * far_share) / total
+        return jnp.dot(attended.astype(jnp.bfloat16), out_w[...], preferred_element_type=jnp.float32)
+
+    for ref in (near_sum, near_top, near_total, far_sum, far_top, far_total):
+        ref[...] = jnp.zeros_like(ref)
+    kv_step(3, 0)
+    attend_near(corner)
+    attend_near(across)
+    kv_step(3, 1)
+    attend_near(near_core)
+    attend_near(own)
+    for distance in range(4, depth):
+        for slot in range(2):
+            kv_step(distance, slot)
+    for load in loads[2:]:
+        load.wait()
+    kv_finish()
+
+    for group in range(groups):
+        for page in range(pages):
+            slot = page_table[group, page]
+            spot = pl.ds((group * pages + page) * page_len, page_len)
+            far_k[spot] = kv_all[slot // 2, slot % 2, 0]
+            far_v[spot] = kv_all[slot // 2, slot % 2, 1]
 
     def to_core(phase, index, part, value):
         where = (phase, index) if part is None else (phase, index, piece(part))
@@ -590,6 +632,24 @@
         copy.wait_send()
     kv_drain()
     cache_out.wait()
+
+
+def hand_over(hidden_in, cache_in, hidden_out, cache_out, hidden_held, cache_held, sems):
+    into = [
+        pltpu.make_async_copy(hidden_in, hidden_held, sems.at[0, 0]),
+        pltpu.make_async_copy(cache_in, cache_held, sems.at[1, 0]),
+    ]
+    out = [
+        pltpu.make_async_copy(hidden_held, hidden_out, sems.at[0, 1]),
+        pltpu.make_async_copy(cache_held, cache_out, sems.at[1, 1]),
+    ]
+    for copy in into:
+        copy.start()
+    for first, then in zip(into, out):
+        first.wait()
+        then.start()
+    for copy in out:
+        copy.wait()
 
 
 def kernel_local(
@@ -629,7 +689,7 @@
         functools.partial(layer_kernel, n_tok),
         out_shape=(
             jax.ShapeDtypeStruct((rows, width), half),
-            jax.ShapeDtypeStruct((2, block_rows, quarter), half),
+            jax.ShapeDtypeStruct((block_rows, 2, quarter), half),
         ),
         in_specs=[
             anywhere, vmem, smem, smem, smem, anywhere, anywhere, vmem, anywhere,
@@ -645,9 +705,15 @@
             pltpu.VMEM((4, rows, width), half),
             pltpu.VMEM((n_tok, slots, 2, page_len, quarter), half),
             pltpu.VMEM((2, block_rows, quarter), half),
+            pltpu.VMEM((block_rows, 2, quarter), half),
             pltpu.VMEM((far_keys, quarter), half),
             pltpu.VMEM((far_keys, quarter), half),
             pltpu.VMEM((block_rows, quarter), half),
+            pltpu.VMEM((block_rows, quarter), jnp.float32),
+            pltpu.VMEM((block_rows, quarter), jnp.float32),
+            pltpu.VMEM((block_rows, quarter), jnp.float32),
+            pltpu.VMEM((rows, quarter), jnp.float32),
+            pltpu.VMEM((rows, quarter), jnp.float32),
             pltpu.VMEM((rows, quarter), jnp.float32),
             pltpu.VMEM((2, 2, rows, width), half),
             pltpu.VMEM((2, 2, rows, width), half),
@@ -690,7 +756,20 @@
         norm2_gain.reshape(1, width),
         norm2_bias.reshape(1, width),
     )
-    return (hidden, kv_out.transpose(1, 0, 2))
+    return pl.pallas_call(
+        hand_over,
+        out_shape=(
+            jax.ShapeDtypeStruct(hidden.shape, half),
+            jax.ShapeDtypeStruct(kv_out.shape, half),
+        ),
+        in_specs=[anywhere, anywhere],
+        out_specs=(anywhere, anywhere),
+        scratch_shapes=[
+            pltpu.VMEM(hidden.shape, half),
+            pltpu.VMEM(kv_out.shape, half),
+            dma((2, 2)),
+        ],
+    )(hidden, kv_out)
 
 
 def solution(mesh):

time: 73 us -> 70.3 us (0.963)
  local copies, waits for them, and re-layouts: 5.72 us -> 1.68 us
  Pallas kernels: 66.4 us -> 67.8 us
    unnamed x3 -> x1, local copies, waits for them, and re-layouts: 5.72 us -> 1.68 us
    pallas_call x0 -> x1, Pallas kernels: none -> 1.95 us  [kernel_local(): pl.pallas_call(hand_over, out_shape=(jax.ShapeDtypeStruct(hidden.shape, h...]
where the time goes in v3:
time: 70.3 us; the launch traced here: 70.1 us
  Pallas kernels  67.8 us (96%)
  local copies, waits for them, and re-layouts  1.68 us (2%)
    pallas_call x1, Pallas kernels, kernel_local(): pl.pallas_call(functools.partial(layer_kernel, n_tok), out_shape=(jax.Sha...  65.8 us
    pallas_call x1, Pallas kernels, kernel_local(): pl.pallas_call(hand_over, out_shape=(jax.ShapeDtypeStruct(hidden.shape, h...  1.95 us
    unnamed x1, local copies, waits for them, and re-layouts  1.68 us

profile of v3, /device:TPU:0, one launch (start us, length us, event | category | flops | bytes accessed | tf_op | source)
XLA Modules:
  0.0 70.1 jit_solution(16403360557140533543)
XLA Ops:
  0.6 1.7 %copy.22 = bf16[2,128,2,256]{3,1,2,0:T(8,128)(2,1)} copy(bf16[2,128,2,256]{3,2,1,0:T(2,128)(2,1)} %param.23) | data formatting | bytes 524288 | tf_op args[5]
  2.3 65.8 %shard_map.185 = (bf16[128,1024]{1,0:T(8,128)(2,1)}, bf16[512,2,256]{2,1,0:T(2,128)(2,1)}) custom-call(bf16[128,1024]{1,0:T(8,128)(2,1)} %tokens.1, s32[1,128]{1,0:T(1,128)} %bitcast.21, s32[1,8]{1,0:T(1,128)} %lengths.1, s32[1,8]{1,0:T(1,128)} %group_ids.1, s32[2,4]{1,0:T(2,128)} %page_table.1, bf16[2,2,128,256]{3,2,1,0:T(8,128)(2,1)} %bitcast.13, ...), custom_call_target="tpu_custom_call" | custom-call | tf_op jit(solution)/shard_map/pallas_call | solution.py:688
  68.1 2.0 %shard_map.186 = (bf16[128,1024]{1,0:T(8,128)(2,1)}, bf16[512,2,256]{2,1,0:T(2,128)(2,1)}) custom-call(bf16[128,1024]{1,0:T(8,128)(2,1)} %get-tuple-element.4.hidden_in, bf16[512,2,256]{2,1,0:T(2,128)(2,1)} %get-tuple-element.5.cache_in), custom_call_target="tpu_custom_call" | custom-call | tf_op jit(solution)/shard_map/pallas_call | solution.py:759
